TPU v7x, 32 devices: a whole 2x2x4 slice. The times are simulated.
32 devices in a mesh: dp: 8 (over z, x), mp: 4 (over y, core).
Axes of the slice: x: 2, y: 2, z: 4, core: 2. Of those that a mesh axis runs over, the one named last changes fastest.
Arguments:
- media: bfloat16 [16, 8, 256, 1024], P('dp'), may hold values from -6 to 6
- latents: bfloat16 [64, 1024], replicated, may hold values from -6 to 6
- time_embed: bfloat16 [8, 1024], replicated, may hold values from -5 to 5
- media_gain: float32 [2, 1024], replicated, may hold values from 0.25 to 1.75
- latent_gain: float32 [2, 1024], replicated, may hold values from 0.25 to 1.75
- ffn_gain: float32 [2, 1024], replicated, may hold values from 0.25 to 1.75
- out_gain: float32 [1024], replicated, may hold values from 0.25 to 1.75
- w_query: bfloat16 [2, 1024, 512], P(None, 'dp', 'mp'), may hold values from -0.1875 to 0.1875
- w_key: bfloat16 [2, 1024, 512], P(None, 'dp', 'mp'), may hold values from -0.1875 to 0.1875
- w_value: bfloat16 [2, 1024, 512], P(None, 'dp', 'mp'), may hold values from -0.1875 to 0.1875
- w_out: bfloat16 [2, 512, 1024], P(None, 'mp', 'dp'), may hold values from -0.25 to 0.25
- w_up: bfloat16 [2, 1024, 4096], P(None, 'dp', 'mp'), may hold values from -0.1875 to 0.1875
- w_down: bfloat16 [2, 4096, 1024], P(None, 'mp', 'dp'), may hold values from -0.09375 to 0.09375
Outputs:
- resampled: bfloat16 [16, 64, 1024], P('dp')
All inputs are finite; a program needn't handle non-finite values.
Results may differ from a plain program's by a relative error of at most 0.013.
Values may be sent and summed in bfloat16 or wider, within the bound.
A program may use at most 128 MiB of HBM per device.

v0:
```python
import jax
import jax.numpy as jnp
from jax import lax
from jax.sharding import PartitionSpec as P

HEAD = 64
LAYERS = 2


def layer_norm(values, gain):
    center = values - jnp.mean(values, axis=-1, keepdims=True)
    spread = jnp.mean(center * center, axis=-1, keepdims=True)
    return center * lax.rsqrt(spread + 1e-05) * gain


def matmul(left, right):
    return jnp.dot(left, right, preferred_element_type=jnp.float32)


def on_device(
    media,
    latents,
    time_embed,
    media_gain,
    latent_gain,
    ffn_gain,
    out_gain,
    w_query,
    w_key,
    w_value,
    w_out,
    w_up,
    w_down,
):
    samples = media.shape[0]
    frames = media.shape[1]
    patches = media.shape[2]
    width = media.shape[3]
    count = latents.shape[0]
    head_size = HEAD
    local_heads = w_query.shape[2] // head_size
    scale = head_size ** (-0.5)
    tokens = frames * patches
    flat = (media.astype(jnp.float32) + time_embed.astype(jnp.float32)[None, :, None, :]).reshape(
        samples * tokens, width
    )
    state = jnp.broadcast_to(latents.astype(jnp.float32)[None], (samples, count, width)).reshape(
        samples * count, width
    )
    row_parts = (
        lax.all_gather(w_query, "dp", axis=1, tiled=True),
        lax.all_gather(w_key, "dp", axis=1, tiled=True),
        lax.all_gather(w_value, "dp", axis=1, tiled=True),
        lax.all_gather(w_up, "dp", axis=1, tiled=True),
    )
    col_parts = (
        lax.all_gather(w_out, "dp", axis=2, tiled=True),
        lax.all_gather(w_down, "dp", axis=2, tiled=True),
    )

    def full_rows(values, gain):
        normed = layer_norm(values, gain).astype(jnp.bfloat16)
        return normed

    def add_update(current, partial_value):
        return current + lax.psum(partial_value.astype(jnp.bfloat16), "mp").astype(jnp.float32)

    for layer in range(LAYERS):
        query_weight = row_parts[0][layer]
        key_weight = row_parts[1][layer]
        value_weight = row_parts[2][layer]
        up_weight = row_parts[3][layer]
        out_weight = col_parts[0][layer]
        down_weight = col_parts[1][layer]
        media_normed = layer_norm(flat, media_gain[layer]).astype(jnp.bfloat16)
        latent_normed = full_rows(state, latent_gain[layer])
        query = matmul(latent_normed, query_weight)
        key_media = matmul(media_normed, key_weight)
        value_media = matmul(media_normed, value_weight)
        key_latent = matmul(latent_normed, key_weight)
        value_latent = matmul(latent_normed, value_weight)
        queries = (
            (query * scale).astype(jnp.bfloat16).reshape(samples, count, local_heads, head_size)
        )
        keys = jnp.concatenate(
            [
                key_media.astype(jnp.bfloat16).reshape(samples, tokens, local_heads, head_size),
                key_latent.astype(jnp.bfloat16).reshape(samples, count, local_heads, head_size),
            ],
            axis=1,
        )
        values = jnp.concatenate(
            [
                value_media.astype(jnp.bfloat16).reshape(samples, tokens, local_heads, head_size),
                value_latent.astype(jnp.bfloat16).reshape(samples, count, local_heads, head_size),
            ],
            axis=1,
        )
        scores = jnp.einsum("sqhd,skhd->shqk", queries, keys, preferred_element_type=jnp.float32)
        probs = jax.nn.softmax(scores, axis=-1).astype(jnp.bfloat16)
        attended = jnp.einsum("shqk,skhd->sqhd", probs, values, preferred_element_type=jnp.float32)
        attended = attended.astype(jnp.bfloat16).reshape(samples * count, local_heads * head_size)
        state = add_update(state, matmul(attended, out_weight))
        ffn_normed = full_rows(state, ffn_gain[layer])
        hidden = jax.nn.gelu(matmul(ffn_normed, up_weight), approximate=False).astype(jnp.bfloat16)
        state = add_update(state, matmul(hidden, down_weight))
    final = layer_norm(state, out_gain).astype(jnp.bfloat16)
    return final.reshape(samples, count, width)


def solution(mesh):
    in_specs = (
        P("dp", None, None, None),
        P(),
        P(),
        P(),
        P(),
        P(),
        P(),
        P(None, "dp", "mp"),
        P(None, "dp", "mp"),
        P(None, "dp", "mp"),
        P(None, "mp", "dp"),
        P(None, "dp", "mp"),
        P(None, "mp", "dp"),
    )
    out_specs = P("dp", None, None)
    return jax.shard_map(
        on_device, mesh=mesh, in_specs=in_specs, out_specs=out_specs, check_vma=False
    )
```

profile of v0, /device:TPU:1, one launch (start us, length us, event | category | flops | bytes accessed | tf_op | source)
XLA Modules:
  0.0 457.1 jit_solution(7624220394603291275)
XLA Ops:
  10.3 27.1 %all_gather.20 = bf16[2,1024,128]{2,1,0:T(8,128)(2,1)S(1)} all-gather(bf16[2,128,128]{2,1,0:T(8,128)(2,1)} %param.21), channel_id=1, replica_groups=mesh['dp'=8,'mp'=4] {'dp'}, dimensions={1}, use_global_device_ids=true | all-gather | bytes 589824 | tf_op jit(solution)/shard_map/all_gather | solution.py:52
  38.2 5.3 %fusion.3 = f32[2,8,256]{2,1,0:T(8,128)S(1)} fusion(bf16[2,8,256,1024]{3,2,1,0:T(8,128)(2,1)} %param.13, f32[8,1024]{1,0:T(8,128)S(1)} %convert_element_type.135), kind=kLoop, calls=%fused_computation.7 | loop fusion | flops 12578816 | bytes 8437760 | tf_op jit(solution)/shard_map/reduce_sum | solution.py:11
  47.6 5.8 %multiply_convert_fusion = (bf16[2,8,256,1024]{3,2,1,0:T(8,128)(2,1)}, bf16[2,8,256,1024]{3,2,1,0:T(8,128)(2,1)S(1)}) fusion(bf16[2,8,256,1024]{3,2,1,0:T(8,128)(2,1)S(1)} %copy-done, f32[1024]{0:T(1024)S(1)} %bitcast.110, f32[2,8,256]{2,1,0:T(8,128)S(1)} %add_rsqrt_fusion, f32[2,8,256]{2,1,0:T(8,128)S(1)} %broadcast_multiply_fusion, ...), kind=kLoop, calls=%fused_computation.2 | loop fusion | flops 33554432 | bytes 25239552 | tf_op jit(solution)/shard_map/convert_element_type | solution.py:75
  56.7 25.4 %all_gather.18 = bf16[2,1024,128]{2,1,0:T(8,128)(2,1)S(1)} all-gather(bf16[2,128,128]{2,1,0:T(8,128)(2,1)S(1)} %copy-done.12), channel_id=1, replica_groups=mesh['dp'=8,'mp'=4] {'dp'}, dimensions={1}, use_global_device_ids=true | all-gather | bytes 589824 | tf_op jit(solution)/shard_map/all_gather | solution.py:53
  86.6 26.0 %all_gather.19 = bf16[2,1024,128]{2,1,0:T(8,128)(2,1)S(1)} all-gather(bf16[2,128,128]{2,1,0:T(8,128)(2,1)S(1)} %copy-done.13), channel_id=1, replica_groups=mesh['dp'=8,'mp'=4] {'dp'}, dimensions={1}, use_global_device_ids=true | all-gather | bytes 589824 | tf_op jit(solution)/shard_map/all_gather | solution.py:51
  113.5 3.9 reshape.424
  117.4 3.5 copy.28
  121.1 3.9 reshape.423
  125.0 3.5 copy.25
  134.3 22.5 %all_gather.21 = bf16[2,128,1024]{2,1,0:T(8,128)(2,1)S(1)} all-gather(bf16[2,128,128]{2,1,0:T(8,128)(2,1)S(1)} %copy-done.14), channel_id=1, replica_groups=mesh['dp'=8,'mp'=4] {'dp'}, dimensions={2}, use_global_device_ids=true | all-gather | bytes 589824 | tf_op jit(solution)/shard_map/all_gather | solution.py:57
  159.8 6.8 %convolution_convert_fusion = bf16[4096,128]{1,0:T(8,128)(2,1)} fusion(bf16[4096,1024]{1,0:T(8,128)(2,1)} %bitcast.100, bf16[2,1024,128]{2,1,0:T(8,128)(2,1)S(1)} %all_gather.20), kind=kOutput, calls=%fused_computation.9 | convolution fusion | flops 1074266112 | bytes 9699328 | tf_op jit(solution)/shard_map/dot_general | solution.py:17
  166.5 43.8 %all-reduce.5.cloned.1.call-done = bf16[128,1024]{1,0:T(8,128)(2,1)} async-done(((bf16[128,1024]{1,0:T(8,128)(2,1)}), bf16[128,1024]{1,0:T(8,128)(2,1)}) %all-reduce.5.cloned.1.call-update) | async-done | bytes 262160 | tf_op jit(solution)/shard_map/psum | solution.py:66
  213.8 39.6 %all-gather.3.cloned.1.call-done = bf16[2,1024,1024]{2,1,0:T(8,128)(2,1)} async-done(((bf16[2,128,1024]{2,1,0:T(8,128)(2,1)}), bf16[2,1024,1024]{2,1,0:T(8,128)(2,1)}) %all-gather.3.cloned.1.call-update) | async-done | bytes 4194320 | tf_op jit(solution)/shard_map/all_gather | solution.py:54
  253.4 75.4 %all-gather.5.cloned.1.call-done = bf16[2,1024,1024]{2,1,0:T(8,128)(2,1)} async-done(((bf16[2,1024,128]{2,1,0:T(8,128)(2,1)}), bf16[2,1024,1024]{2,1,0:T(8,128)(2,1)}) %all-gather.5.cloned.1.call-update) | async-done | bytes 4194320 | tf_op jit(solution)/shard_map/all_gather | solution.py:58
  328.8 4.8 %fusion.13 = bf16[128,1024]{1,0:T(8,128)(2,1)} fusion(bf16[2,1024,1024]{2,1,0:T(8,128)(2,1)} %all-gather.5.cloned.1.call-done, bf16[128,1024]{1,0:T(8,128)(2,1)S(1)} %multiply_convert_fusion.5, bf16[2,1024,1024]{2,1,0:T(8,128)(2,1)} %all-gather.3.cloned.1.call-done), kind=kOutput, calls=%fused_computation.27 | convolution fusion | flops 545521664 | bytes 4718592 | tf_op jit(solution)/shard_map/dot_general | solution.py:17
  333.9 6.7 %convolution_convert_fusion.1 = bf16[4096,128]{1,0:T(8,128)(2,1)} fusion(bf16[4096,1024]{1,0:T(8,128)(2,1)} %bitcast.101, bf16[2,1024,128]{2,1,0:T(8,128)(2,1)S(1)} %copy-done.4), kind=kOutput, calls=%fused_computation.10 | convolution fusion | flops 1074266112 | bytes 9699328 | tf_op jit(solution)/shard_map/dot_general | solution.py:17
  340.6 3.9 reshape.426
  344.5 3.5 copy.36
  348.0 3.9 reshape.425
  351.9 3.6 copy.33
  355.5 8.0 %all-reduce.7.cloned.1.call-done = bf16[128,1024]{1,0:T(8,128)(2,1)} async-done(((bf16[128,1024]{1,0:T(8,128)(2,1)}), bf16[128,1024]{1,0:T(8,128)(2,1)}) %all-reduce.7.cloned.1.call-update) | async-done | bytes 262160 | tf_op jit(solution)/shard_map/psum | solution.py:66
  374.8 32.4 %all-reduce.9.cloned.1.call-done = bf16[128,1024]{1,0:T(8,128)(2,1)} async-done(((bf16[128,1024]{1,0:T(8,128)(2,1)}), bf16[128,1024]{1,0:T(8,128)(2,1)}) %all-reduce.9.cloned.1.call-update) | async-done | bytes 262160 | tf_op jit(solution)/shard_map/psum | solution.py:66
  408.6 4.8 %fusion.14 = bf16[128,1024]{1,0:T(8,128)(2,1)} fusion(bf16[2,1024,1024]{2,1,0:T(8,128)(2,1)} %all-gather.5.cloned.1.call-done, bf16[2,1024,1024]{2,1,0:T(8,128)(2,1)} %all-gather.3.cloned.1.call-done, f32[128,1024]{1,0:T(8,128)S(1)} %get-tuple-element.6, f32[1024]{0:T(1024)S(1)} %bitcast.112, f32[128]{0:T(128)S(1)} %add_rsqrt_fusion.3, ...), kind=kOutput, calls=%fused_computation.28 | convolution fusion | flops 546045952 | bytes 4985856 | tf_op jit(solution)/shard_map/dot_general | solution.py:17
  413.5 32.4 %all-reduce.11.cloned.1.call-done = bf16[128,1024]{1,0:T(8,128)(2,1)} async-done(((bf16[128,1024]{1,0:T(8,128)(2,1)}), bf16[128,1024]{1,0:T(8,128)(2,1)}) %all-reduce.11.cloned.1.call-update) | async-done | bytes 262160 | tf_op jit(solution)/shard_map/psum | solution.py:66
  (108 shorter events, 45.7 us)
Async XLA Ops:
  7.4 203.0 %all-reduce.5.cloned.1.call-start = ((), (), s32[]{:S(2)}) async-start(), calls=%async_computation | async-start | bytes 524288 | tf_op jit(solution)/shard_map/psum | solution.py:66
  38.2 5.8 %copy-start = (bf16[2,8,256,1024]{3,2,1,0:T(8,128)(2,1)S(1)}, bf16[2,8,256,1024]{3,2,1,0:T(8,128)(2,1)}, u32[]{:S(2)}) copy-start(bf16[2,8,256,1024]{3,2,1,0:T(8,128)(2,1)} %param.13) | copy-start | bytes 25165828
  44.0 3.2 copy-start.15
  53.3 3.4 copy-start.12
  82.1 0.8 copy-start.3
  82.9 3.7 copy-start.13
  112.6 0.8 copy-start.10
  128.6 3.4 copy-start.9
  131.9 2.4 copy-start.14
  134.1 25.6 %copy-start.16 = (f32[2,1024]{1,0:T(2,128)S(1)}, f32[2,1024]{1,0:T(2,128)}, u32[]{:S(2)}) copy-start(f32[2,1024]{1,0:T(2,128)} %param.18) | copy-start | bytes 24580
  156.8 0.8 copy-start.6
  158.5 94.9 %all-gather.3.cloned.1.call-start = ((), (), s32[]{:S(2)}) async-start(), calls=%async_computation.1 | async-start | bytes 4718592 | tf_op jit(solution)/shard_map/all_gather | solution.py:54
  159.1 169.7 %all-gather.5.cloned.1.call-start = ((), (), s32[]{:S(2)}) async-start(), calls=%async_computation.2 | async-start | bytes 4718592 | tf_op jit(solution)/shard_map/all_gather | solution.py:58
  159.7 203.8 %all-reduce.7.cloned.1.call-start = ((), (), s32[]{:S(2)}) async-start(), calls=%async_computation.3 | async-start | bytes 524288 | tf_op jit(solution)/shard_map/psum | solution.py:66
  213.7 120.2 %copy-start.4 = (bf16[2,1024,128]{2,1,0:T(8,128)(2,1)S(1)}, bf16[2,1024,128]{2,1,0:T(8,128)(2,1)}, u32[]{:S(2)}) copy-start(bf16[2,1024,128]{2,1,0:T(8,128)(2,1)} %copy-done.3) | copy-start | bytes 1572868
  333.6 73.6 %all-reduce.9.cloned.1.call-start = ((), (), s32[]{:S(2)}) async-start(), calls=%async_computation.4 | async-start | bytes 524288 | tf_op jit(solution)/shard_map/psum | solution.py:66
  351.9 11.6 %copy-start.1 = (bf16[128,1024]{1,0:T(8,128)(2,1)S(1)}, bf16[128,1024]{1,0:T(8,128)(2,1)}, u32[]{:S(2)}) copy-start(bf16[128,1024]{1,0:T(8,128)(2,1)} %all-reduce.5.cloned.1.call-done) | copy-start | bytes 786436
  355.5 11.6 %copy-start.11 = (bf16[2,1024,128]{2,1,0:T(8,128)(2,1)S(1)}, bf16[2,1024,128]{2,1,0:T(8,128)(2,1)}, u32[]{:S(2)}) copy-start(bf16[2,1024,128]{2,1,0:T(8,128)(2,1)} %copy-done.10) | copy-start | bytes 1572868
  355.5 11.9 %copy-start.5 = (bf16[2,1024,128]{2,1,0:T(8,128)(2,1)S(1)}, bf16[2,1024,128]{2,1,0:T(8,128)(2,1)}, u32[]{:S(2)}) copy-start(bf16[2,1024,128]{2,1,0:T(8,128)(2,1)} %copy-done.3) | copy-start | bytes 1572868
  367.6 3.8 copy-start.8
  371.4 2.5 copy-start.7
  371.4 35.8 %copy-start.2 = (bf16[128,1024]{1,0:T(8,128)(2,1)S(1)}, bf16[128,1024]{1,0:T(8,128)(2,1)}, u32[]{:S(2)}) copy-start(bf16[128,1024]{1,0:T(8,128)(2,1)} %all-reduce.7.cloned.1.call-done) | copy-start | bytes 786436
  374.8 71.1 %all-reduce.11.cloned.1.call-start = ((), (), s32[]{:S(2)}) async-start(), calls=%async_computation.5 | async-start | bytes 524288 | tf_op jit(solution)/shard_map/psum | solution.py:66
  408.6 39.6 %copy-start.17 = (f32[1024]{0:T(1024)S(1)}, f32[1024]{0:T(1024)}, u32[]{:S(2)}) copy-start(f32[1024]{0:T(1024)} %param.19) | copy-start | bytes 12292
Sparse Core Ops, SparseCore 0:
  158.7 51.6 all-reduce.4
  333.7 29.6 all-reduce.6
  374.9 32.2 all-reduce.8
  413.6 32.2 all-reduce.10
Sparse Core Ops, SparseCore 1:
  161.2 92.1 all-gather.2
  255.3 73.5 all-gather.4
where the time goes:
time: 460 us; the launch traced here: 457 us
  waiting for transfers between devices  233 us (51%)
  blocking collectives  101 us (22%)
  matrix products  44.2 us (10%)
  local copies, waits for them, and re-layouts  34.3 us (7%)
  other arithmetic  29.4 us (6%)
  between operations  15 us (3%)
    psum x4, waiting for transfers between devices, add_update(): lax.psum(partial_value.astype(jnp.bfloat16), 'mp').astype(jnp.float32)  117 us
    all_gather x1, waiting for transfers between devices, on_device(): lax.all_gather(w_down, 'dp', axis=2, tiled=True)  75.4 us
    all_gather x1, waiting for transfers between devices, on_device(): lax.all_gather(w_up, 'dp', axis=1, tiled=True)  39.6 us
    dot_general x14, matrix products, matmul(): return jnp.dot(left, right, preferred_element_type=jnp.float32)  33.2 us
    all_gather x1, blocking collectives, on_device(): lax.all_gather(w_key, 'dp', axis=1, tiled=True)  27.1 us
    all_gather x1, blocking collectives, on_device(): lax.all_gather(w_query, 'dp', axis=1, tiled=True)  26 us
    all_gather x1, blocking collectives, on_device(): lax.all_gather(w_value, 'dp', axis=1, tiled=True)  25.4 us
    all_gather x1, blocking collectives, on_device(): lax.all_gather(w_out, 'dp', axis=2, tiled=True)  22.5 us
  transfers between devices with their start and end apart: 6, of which 6 were waited for; matrix products, arithmetic and copies ran while one was open for 7% of the time, Pallas kernels for 0%

commit v1 on v0

--- a/solution.py
+++ b/solution.py
@@ -1,7 +1,13 @@
+import functools
+
 import jax
 import jax.numpy as jnp
 from jax import lax
+from jax.experimental import pallas as pl
+from jax.experimental.pallas import tpu as pltpu
 from jax.sharding import PartitionSpec as P
+
+MESH = pl.DeviceIdType.MESH
 
 HEAD = 64
 LAYERS = 2
@@ -108,6 +114,336 @@
     return final.reshape(samples, count, width)
 
 
+def fused_kernel(
+    n, groups,
+    media, latents, time_embed, media_gain, latent_gain, ffn_gain, out_gain,
+    w_query, w_key, w_value, w_out, w_up, w_down,
+    out,
+    frames_in, normed_next, kv, g_qkv, g_out, g_up, g_down, state,
+    part, rs_in, ag_in,
+    media_sem, own_sem, send_sem, recv_sem, rs_send, rs_recv, ag_send, ag_recv,
+):
+    samples, frames, patches, width = media.shape
+    count = latents.shape[0]
+    tokens = frames * patches
+    inner = w_query.shape[2]
+    heads = inner // HEAD
+    depth = w_query.shape[1]
+    hidden = w_up.shape[2]
+    half = hidden // 2
+    ring = n // 2
+    me = lax.axis_index("dp")
+    mine = lax.axis_index("mp")
+    along, across = me // 2, me % 2
+
+    def index(a, b):
+        return lax.rem(a + 2 * ring, ring) * 2 + b
+
+    for target in (index(along, 1 - across), index(along + 1, across), index(along - 1, across)):
+        pl.semaphore_signal(pltpu.get_barrier_semaphore(), inc=1, device_id={"dp": target}, device_id_type=MESH)
+    for k in range(1, groups):
+        pl.semaphore_signal(
+            pltpu.get_barrier_semaphore(), inc=1, device_id={"mp": lax.rem(mine + k, groups)}, device_id_type=MESH
+        )
+
+    units = []
+    for layer in range(LAYERS):
+        if layer == 0:
+            units += [("qkv", 0, 0), ("qkv", 1, 1)]
+        units += [("out", layer, layer), ("up", layer, 0), ("up", layer, 1), ("down", layer, 0), ("down", layer, 1)]
+    where = {unit: i for i, unit in enumerate(units)}
+
+    def span(origin, size):
+        return pl.ds(pl.multiple_of(origin * size, size), size)
+
+    def piece(u, origin):
+        kind, layer, part_of = units[u]
+        if kind == "qkv":
+            return g_qkv.at[layer, span(origin, depth), :]
+        if kind == "out":
+            return g_out.at[layer, :, span(origin, depth)]
+        if kind == "up":
+            return g_up.at[layer, span(origin, depth), pl.ds(part_of * half, half)]
+        return g_down.at[layer, pl.ds(part_of * half, half), span(origin, depth)]
+
+    def own_copies(u):
+        kind, layer, part_of = units[u]
+        if kind == "qkv":
+            return [
+                pltpu.make_async_copy(
+                    w.at[layer], g_qkv.at[layer, span(me, depth), pl.ds(i * inner, inner)], own_sem.at[u, i]
+                )
+                for i, w in enumerate((w_query, w_key, w_value))
+            ]
+        if kind == "out":
+            source = w_out.at[layer]
+        elif kind == "up":
+            source = w_up.at[layer, :, pl.ds(part_of * half, half)]
+        else:
+            source = w_down.at[layer, pl.ds(part_of * half, half), :]
+        return [pltpu.make_async_copy(source, piece(u, me), own_sem.at[u, 0])]
+
+    def turn(u):
+        return 1 if units[u][2] == 0 else -1
+
+    def sending(u, s, other, to_ring):
+        r = turn(u)
+        ref = piece(u, index(along - r * s, 1 - across if other else across))
+        if to_ring:
+            target, slot = index(along + r, across), recv_sem.at[u, s + 1, other]
+        else:
+            target, slot = index(along, 1 - across), recv_sem.at[u, s, 1 - other]
+        return pltpu.make_async_remote_copy(
+            src_ref=ref, dst_ref=ref, send_sem=send_sem.at[u, s, other, int(to_ring)], recv_sem=slot,
+            device_id={"dp": target}, device_id_type=MESH,
+        )
+
+    started = []
+
+    def send(*which):
+        copy = sending(*which)
+        copy.start()
+        started.append(copy)
+
+    def arrived(u, s, other):
+        r = turn(u)
+        ref = piece(u, index(along - r * s, 1 - across if other else across))
+        pltpu.make_async_remote_copy(
+            src_ref=ref, dst_ref=ref, send_sem=send_sem.at[u, s, other, 0], recv_sem=recv_sem.at[u, s, other],
+            device_id={"dp": index(along, 1 - across)}, device_id_type=MESH,
+        ).wait_recv()
+
+    def pair_first(u):
+        return units[u][0] == "up" and units[u][2] == 1
+
+    def event(u, s):
+        if s == 0:
+            for copy in own_copies(u):
+                copy.wait()
+            send(u, 0, 0, True)
+            send(u, 0, 0, False)
+            return
+        if pair_first(u):
+            arrived(u, s - 1, 1)
+            send(u, s - 1, 1, True)
+            arrived(u, s, 0)
+            if s < ring - 1:
+                send(u, s, 0, True)
+        else:
+            arrived(u, s, 0)
+            if s < ring - 1:
+                send(u, s, 0, True)
+            send(u, s, 0, False)
+
+    def complete(u):
+        if pair_first(u):
+            arrived(u, ring - 1, 1)
+        else:
+            for s in range(ring):
+                arrived(u, s, 1)
+
+    slots = {}
+    for u in range(len(units)):
+        for s in range(ring):
+            slots.setdefault(u + s + (1 if s else 0), []).append((u, s))
+    clock = [0]
+
+    def advance(until):
+        while clock[0] <= until:
+            for u, s in sorted(slots.get(clock[0], []), key=lambda e: (e[1] > 0, e[0])):
+                event(u, s)
+            clock[0] += 1
+
+    def need(*unit):
+        u = where[unit]
+        advance(u + ring)
+        complete(u)
+
+    for u in range(len(units)):
+        for copy in own_copies(u):
+            copy.start()
+
+    def frame_copy(i):
+        return pltpu.make_async_copy(media.at[i // frames, i % frames], frames_in.at[i], media_sem.at[i])
+
+    @pl.loop(0, samples * frames)
+    def _(i):
+        frame_copy(i).start()
+
+    pl.semaphore_wait(pltpu.get_barrier_semaphore(), 3 + groups - 1)
+    advance(1)
+
+    state[...] = jnp.concatenate([latents[...].astype(jnp.float32)] * samples, axis=0)
+
+    def norm_frames(low, high):
+        @pl.loop(low, high)
+        def _(i):
+            frame_copy(i).wait()
+
+            @pl.loop(0, patches // 64)
+            def _(j):
+                rows = pl.ds(pl.multiple_of(j * 64, 64), 64)
+                flat = frames_in[i, rows, :].astype(jnp.float32) + time_embed[pl.ds(lax.rem(i, frames), 1), :]
+                center = flat - jnp.mean(flat, axis=-1, keepdims=True)
+                spread = jnp.mean(center * center, axis=-1, keepdims=True)
+                scaled = center * lax.rsqrt(spread + 1e-05)
+                frames_in[i, rows, :] = (scaled * media_gain[0:1, :]).astype(jnp.bfloat16)
+                normed_next[i, rows, :] = (scaled * media_gain[1:2, :]).astype(jnp.bfloat16)
+
+    def project(layer):
+        normed = frames_in if layer == 0 else normed_next
+
+        @pl.loop(0, samples * frames)
+        def _(i):
+            both = matmul(normed[i], g_qkv[layer, :, inner : 3 * inner])
+            rows = pl.ds(pl.multiple_of(lax.rem(i, frames) * patches, patches), patches)
+            kv[layer, i // frames, rows, :] = both.astype(jnp.bfloat16)
+
+    def attend(layer):
+        normed = layer_norm(state[...], latent_gain[layer : layer + 1, :]).astype(jnp.bfloat16)
+        own = matmul(normed, g_qkv[layer])
+        queries = (own[:, :inner] * (HEAD ** (-0.5))).astype(jnp.bfloat16)
+        own_kv = own[:, inner:].astype(jnp.bfloat16)
+        lane = lax.broadcasted_iota(jnp.int32, (count, inner), 1) // HEAD
+        dims = (((1,), (1,)), ((), ()))
+        results = []
+        for b in range(samples):
+            q = queries[b * count : (b + 1) * count]
+            stacked = jnp.concatenate([jnp.where(lane == h, q, jnp.zeros_like(q)) for h in range(heads)], axis=0)
+            k_own = own_kv[b * count : (b + 1) * count, :inner]
+            v_own = own_kv[b * count : (b + 1) * count, inner:]
+            s_far = lax.dot_general(stacked, kv[layer, b, :, :inner], dims, preferred_element_type=jnp.float32)
+            s_own = lax.dot_general(stacked, k_own, dims, preferred_element_type=jnp.float32)
+            top = jnp.maximum(jnp.max(s_far, axis=-1, keepdims=True), jnp.max(s_own, axis=-1, keepdims=True))
+            e_far, e_own = jnp.exp(s_far - top), jnp.exp(s_own - top)
+            total = jnp.sum(e_far, axis=-1, keepdims=True) + jnp.sum(e_own, axis=-1, keepdims=True)
+            inverse = 1.0 / total
+            mixed = matmul((e_far * inverse).astype(jnp.bfloat16), kv[layer, b, :, inner:])
+            mixed += matmul((e_own * inverse).astype(jnp.bfloat16), v_own)
+            result = mixed[:count]
+            for h in range(1, heads):
+                result = jnp.where(lane == h, mixed[h * count : (h + 1) * count], result)
+            results.append(result.astype(jnp.bfloat16))
+        return jnp.concatenate(results, axis=0)
+
+    rows_each = samples * count // groups
+
+    def add_update(a, update):
+        part[a] = update.astype(jnp.bfloat16).reshape(groups, rows_each, width)
+        first = []
+        for k in range(1, groups):
+            peer = lax.rem(mine + k, groups)
+            copy = pltpu.make_async_remote_copy(
+                src_ref=part.at[a, peer], dst_ref=rs_in.at[a, k - 1],
+                send_sem=rs_send.at[a, k - 1], recv_sem=rs_recv.at[a, k - 1],
+                device_id={"mp": peer}, device_id_type=MESH,
+            )
+            copy.start()
+            started.append(copy)
+            first.append(copy)
+        total = part[a, mine].astype(jnp.float32)
+        for k, copy in enumerate(first):
+            copy.wait_recv()
+            total += rs_in[a, k].astype(jnp.float32)
+        ag_in[a, mine] = total.astype(jnp.bfloat16)
+        second = []
+        for k in range(1, groups):
+            copy = pltpu.make_async_remote_copy(
+                src_ref=ag_in.at[a, mine], dst_ref=ag_in.at[a, mine],
+                send_sem=ag_send.at[a, k - 1], recv_sem=ag_recv.at[a, k - 1],
+                device_id={"mp": lax.rem(mine + k, groups)}, device_id_type=MESH,
+            )
+            copy.start()
+            started.append(copy)
+            second.append(copy)
+        for copy in second:
+            copy.wait_recv()
+        state[...] += ag_in[a].astype(jnp.float32).reshape(samples * count, width)
+
+    middle = samples * frames // 2
+    norm_frames(0, middle)
+    advance(2)
+    norm_frames(middle, samples * frames)
+    for layer in range(LAYERS):
+        if layer == 0:
+            need("qkv", 0, 0)
+            project(0)
+        attended = attend(layer)
+        if layer == 0:
+            need("qkv", 1, 1)
+            project(1)
+        need("out", layer, layer)
+        add_update(2 * layer, matmul(attended, g_out[layer]))
+        normed = layer_norm(state[...], ffn_gain[layer : layer + 1, :]).astype(jnp.bfloat16)
+        active = []
+        for h in range(2):
+            need("up", layer, h)
+            value = matmul(normed, g_up[layer, :, h * half : (h + 1) * half])
+            active.append((0.5 * value * (1.0 + lax.erf(value * (0.5**0.5)))).astype(jnp.bfloat16))
+        update = None
+        for h in range(2):
+            need("down", layer, h)
+            term = matmul(active[h], g_down[layer, h * half : (h + 1) * half, :])
+            update = term if update is None else update + term
+        add_update(2 * layer + 1, update)
+    final = layer_norm(state[...], out_gain[...]).astype(jnp.bfloat16)
+    out[...] = final.reshape(samples, count, width)
+    for copy in started:
+        copy.wait_send()
+
+
+def fused(n, groups, media, latents, time_embed, media_gain, latent_gain, ffn_gain, out_gain,
+          w_query, w_key, w_value, w_out, w_up, w_down):
+    samples, frames, patches, width = media.shape
+    count = latents.shape[0]
+    inner = w_query.shape[2]
+    hidden = w_up.shape[2]
+    ring = n // 2
+    rows_each = samples * count // groups
+    units = LAYERS * 6
+    bf16 = jnp.bfloat16
+    dma = pltpu.SemaphoreType.DMA
+    anywhere = pl.BlockSpec(memory_space=pl.ANY)
+    local = pl.BlockSpec(memory_space=pltpu.VMEM)
+    return pl.pallas_call(
+        functools.partial(fused_kernel, n, groups),
+        out_shape=jax.ShapeDtypeStruct((samples, count, width), bf16),
+        in_specs=[anywhere] + [local] * 6 + [anywhere] * 6,
+        out_specs=local,
+        scratch_shapes=[
+            pltpu.VMEM((samples * frames, patches, width), bf16),
+            pltpu.VMEM((samples * frames, patches, width), bf16),
+            pltpu.VMEM((LAYERS, samples, frames * patches, 2 * inner), bf16),
+            pltpu.VMEM((LAYERS, width, 3 * inner), bf16),
+            pltpu.VMEM((LAYERS, inner, width), bf16),
+            pltpu.VMEM((LAYERS, width, hidden), bf16),
+            pltpu.VMEM((LAYERS, hidden, width), bf16),
+            pltpu.VMEM((samples * count, width), jnp.float32),
+            pltpu.VMEM((2 * LAYERS, groups, rows_each, width), bf16),
+            pltpu.VMEM((2 * LAYERS, groups - 1, rows_each, width), bf16),
+            pltpu.VMEM((2 * LAYERS, groups, rows_each, width), bf16),
+            dma((samples * frames,)),
+            dma((units, 3)),
+            dma((units, ring, 2, 2)),
+            dma((units, ring, 2)),
+            dma((2 * LAYERS, groups - 1)),
+            dma((2 * LAYERS, groups - 1)),
+            dma((2 * LAYERS, groups - 1)),
+            dma((2 * LAYERS, groups - 1)),
+        ],
+        compiler_params=pltpu.CompilerParams(
+            collective_id=0, has_side_effects=True, vmem_limit_bytes=60 * 2**20
+        ),
+    )(media, latents, time_embed.astype(jnp.float32), media_gain, latent_gain, ffn_gain, out_gain[None],
+      w_query, w_key, w_value, w_out, w_up, w_down)
+
+
+def choose(n, groups, *args):
+    if n >= 4 and n % 2 == 0 and args[7].shape[1] % 128 == 0 and args[7].shape[2] == 128:
+        return fused(n, groups, *args)
+    return on_device(*args)
+
+
 def solution(mesh):
     in_specs = (
         P("dp", None, None, None),
@@ -125,6 +461,7 @@
         P(None, "mp", "dp"),
     )
     out_specs = P("dp", None, None)
+    body = functools.partial(choose, mesh.shape["dp"], mesh.shape["mp"])
     return jax.shard_map(
-        on_device, mesh=mesh, in_specs=in_specs, out_specs=out_specs, check_vma=False
-    )
+        body, mesh=mesh, in_specs=in_specs, out_specs=out_specs, check_vma=False
+    )

time: 460 us -> 170 us (0.37)
  waiting for transfers between devices: 233 us -> 0 us
  Pallas kernels: 0 us -> 167 us
  blocking collectives: 101 us -> 0 us
  matrix products: 44.2 us -> 0 us
  local copies, waits for them, and re-layouts: 34.3 us -> 1.67 us
  other arithmetic: 29.4 us -> 1.33 us
  between operations: 15 us -> 0.01 us
    pallas_call x0 -> x1, Pallas kernels: none -> 167 us  [fused(): pl.pallas_call(functools.partial(fused_kernel, n, groups), out_shape=jax....]
    psum x4 -> x0, waiting for transfers between devices: 117 us -> none  [add_update(): lax.psum(partial_value.astype(jnp.bfloat16), 'mp').astype(jnp.float32)]
    all_gather x2 -> x0, waiting for transfers between devices: 115 us -> none  [the longest x1 75.4 us: on_device(): lax.all_gather(w_down, 'dp', axis=2, tiled=True)]
    all_gather x4 -> x0, blocking collectives: 101 us -> none  [the longest x1 27.1 us: on_device(): lax.all_gather(w_key, 'dp', axis=1, tiled=True)]
    dot_general x16 -> x0, matrix products: 37.6 us -> none  [the longest x14 33.2 us: matmul(): return jnp.dot(left, right, preferred_element_type=jnp.float32)]
    reshape x20 -> x0, local copies, waits for them, and re-layouts: 30.8 us -> none  [the longest x4 14.9 us: on_device(): value_media.astype(jnp.bfloat16)]
    reduce_sum x12 -> x0, other arithmetic: 17.8 us -> none  [the longest x6 10.7 us: layer_norm(): center = values - jnp.mean(values, axis=-1, keepdims=True)]
    convert_element_type x7 -> x1, other arithmetic: 11.6 us -> 1.33 us  [fused(): time_embed.astype(jnp.float32)]
  transfers between devices with their start and end apart: 6 -> 0, of which waited for: 6 -> 0; matrix products, arithmetic and copies ran while one was open for 7% -> 0% of each run, Pallas kernels for 0% -> 0%
where the time goes in v1:
time: 170 us
  Pallas kernels  167 us (98%)
    pallas_call x1, Pallas kernels, fused(): pl.pallas_call(functools.partial(fused_kernel, n, groups), out_shape=jax....  167 us

profile of v1, /device:TPU:1, one launch (start us, length us, event | category | flops | bytes accessed | tf_op | source)
XLA Modules:
  0.0 170.0 jit_solution(11753489712247970980)
XLA Ops:
  0.0 1.3 convert_element_type.3.time_embed
  1.3 166.9 %shard_map.127 = bf16[2,64,1024]{2,1,0:T(8,128)(2,1)} custom-call(bf16[2,8,256,1024]{3,2,1,0:T(8,128)(2,1)} %media.1, bf16[64,1024]{1,0:T(8,128)(2,1)} %latents.1, f32[8,1024]{1,0:T(8,128)} %convert_element_type.3.time_embed, f32[2,1024]{1,0:T(2,128)} %media_gain.1, f32[2,1024]{1,0:T(2,128)} %latent_gain.1, f32[2,1024]{1,0:T(2,128)} %ffn_gain.1, ...), custom_call_target="tpu_custom_call" | custom-call | tf_op jit(solution)/shard_map/pallas_call | solution.py:408
  168.3 1.7 copy.15

commit v2 on v1

--- a/solution.py
+++ b/solution.py
@@ -11,6 +11,9 @@
 
 HEAD = 64
 LAYERS = 2
+LEAD = 1
+PARTS = 4
+AHEAD = 2
 
 
 def layer_norm(values, gain):
@@ -245,7 +248,7 @@
     slots = {}
     for u in range(len(units)):
         for s in range(ring):
-            slots.setdefault(u + s + (1 if s else 0), []).append((u, s))
+            slots.setdefault(u + s + 0 if s else max(0, u - LEAD), []).append((u, s))
     clock = [0]
 
     def advance(until):
@@ -256,7 +259,7 @@
 
     def need(*unit):
         u = where[unit]
-        advance(u + ring)
+        advance(u + ring - 1 + 0 + AHEAD)
         complete(u)
 
     for u in range(len(units)):
@@ -271,7 +274,7 @@
         frame_copy(i).start()
 
     pl.semaphore_wait(pltpu.get_barrier_semaphore(), 3 + groups - 1)
-    advance(1)
+    advance(0)
 
     state[...] = jnp.concatenate([latents[...].astype(jnp.float32)] * samples, axis=0)
 
@@ -341,6 +344,7 @@
             copy.start()
             started.append(copy)
             first.append(copy)
+        advance(clock[0])
         total = part[a, mine].astype(jnp.float32)
         for k, copy in enumerate(first):
             copy.wait_recv()
@@ -356,14 +360,15 @@
             copy.start()
             started.append(copy)
             second.append(copy)
+        advance(clock[0])
         for copy in second:
             copy.wait_recv()
         state[...] += ag_in[a].astype(jnp.float32).reshape(samples * count, width)
 
-    middle = samples * frames // 2
-    norm_frames(0, middle)
-    advance(2)
-    norm_frames(middle, samples * frames)
+    block = samples * frames // PARTS
+    for i in range(PARTS):
+        norm_frames(i * block, (i + 1) * block)
+        advance(i + 1)
     for layer in range(LAYERS):
         if layer == 0:
             need("qkv", 0, 0)

time: 170 us -> 142 us (0.84)
  the two profiles are of different devices: /device:TPU:1 before, /device:TPU:23 now
where the time goes in v2:
time: 142 us
  Pallas kernels  139 us (98%)
  local copies, waits for them, and re-layouts  1.67 us (1%)
    pallas_call x1, Pallas kernels, fused(): pl.pallas_call(functools.partial(fused_kernel, n, groups), out_shape=jax....  139 us

profile of v2, /device:TPU:23, one launch (start us, length us, event | category | flops | bytes accessed | tf_op | source)
XLA Modules:
  0.0 142.2 jit_solution(8798432290880801768)
XLA Ops:
  0.0 1.3 convert_element_type.3.time_embed
  1.3 139.1 %shard_map.127 = bf16[2,64,1024]{2,1,0:T(8,128)(2,1)} custom-call(bf16[2,8,256,1024]{3,2,1,0:T(8,128)(2,1)} %media.1, bf16[64,1024]{1,0:T(8,128)(2,1)} %latents.1, f32[8,1024]{1,0:T(8,128)} %convert_element_type.3.time_embed, f32[2,1024]{1,0:T(2,128)} %media_gain.1, f32[2,1024]{1,0:T(2,128)} %latent_gain.1, f32[2,1024]{1,0:T(2,128)} %ffn_gain.1, ...), custom_call_target="tpu_custom_call" | custom-call | tf_op jit(solution)/shard_map/pallas_call | solution.py:413
  140.5 1.7 %copy.15 = bf16[2,64,1024]{2,1,0:T(8,128)(2,1)} copy(bf16[2,64,1024]{2,1,0:T(8,128)(2,1)} %shard_map.127) | data formatting | bytes 524288

commit v3 on v2

--- a/solution.py
+++ b/solution.py
@@ -187,7 +187,7 @@
         return [pltpu.make_async_copy(source, piece(u, me), own_sem.at[u, 0])]
 
     def turn(u):
-        return 1 if units[u][2] == 0 else -1
+        return 1
 
     def sending(u, s, other, to_ring):
         r = turn(u)

time: 142 us -> 136 us (0.958)
  the two profiles are of different devices: /device:TPU:23 before, /device:TPU:1 now
where the time goes in v3:
time: 136 us
  Pallas kernels  133 us (98%)
  local copies, waits for them, and re-layouts  1.67 us (1%)
    pallas_call x1, Pallas kernels, fused(): pl.pallas_call(functools.partial(fused_kernel, n, groups), out_shape=jax....  133 us

profile of v3, /device:TPU:1, one launch (start us, length us, event | category | flops | bytes accessed | tf_op | source)
XLA Modules:
  0.0 136.2 jit_solution(6987305777510115526)
XLA Ops:
  0.0 1.3 convert_element_type.3.time_embed
  1.3 133.2 %shard_map.127 = bf16[2,64,1024]{2,1,0:T(8,128)(2,1)} custom-call(bf16[2,8,256,1024]{3,2,1,0:T(8,128)(2,1)} %media.1, bf16[64,1024]{1,0:T(8,128)(2,1)} %latents.1, f32[8,1024]{1,0:T(8,128)} %convert_element_type.3.time_embed, f32[2,1024]{1,0:T(2,128)} %media_gain.1, f32[2,1024]{1,0:T(2,128)} %latent_gain.1, f32[2,1024]{1,0:T(2,128)} %ffn_gain.1, ...), custom_call_target="tpu_custom_call" | custom-call | tf_op jit(solution)/shard_map/pallas_call | solution.py:413
  134.6 1.7 %copy.15 = bf16[2,64,1024]{2,1,0:T(8,128)(2,1)} copy(bf16[2,64,1024]{2,1,0:T(8,128)(2,1)} %shard_map.127) | data formatting | bytes 524288
